TPU v7x, 32 devices: a whole 2x2x4 slice. The times are simulated.
32 devices in a mesh: dp: 4 (over y, core), row: 2 (over x), col: 4 (over z).
Axes of the slice: x: 2, y: 2, z: 4, core: 2. Of those that a mesh axis runs over, the one named last changes fastest.
Arguments:
- tokens: bfloat16 [16384, 1152], P(('dp', 'col')), may hold values from -6 to 6
- segment_ids: int32 [16384], P(('dp', 'col')), may hold values from -1 to 10, as said below
- doc_starts: int32 [4, 12], P('dp'), may hold values from 0 to 4096, as said below
- norm1_gain: bfloat16 [1152], P('col'), may hold values from 0.25 to 1.75
- norm2_gain: bfloat16 [1152], P('col'), may hold values from 0.25 to 1.75
- query_key_value_weight: bfloat16 [1152, 6, 320], P('col', 'row'), may hold values from -0.1875 to 0.1875
- output_weight: bfloat16 [1152, 6, 192], P('col', 'row'), may hold values from -2 to 2
- w_gate_up: bfloat16 [1152, 2, 3072], P('col', None, 'row'), may hold values from -0.1875 to 0.1875
- w_down: bfloat16 [1152, 3072], P('col', 'row'), may hold values from -0.21875 to 0.21875
- cotangent: bfloat16 [16384, 1152], P(('dp', 'col')), may hold values from -6 to 6
Outputs:
- layer_output: bfloat16 [16384, 1152], P(('dp', 'col'))
- input_grad: float32 [16384, 1152], P(('dp', 'col'))
- norm1_gain_grad: float32 [1152], P('col')
- norm2_gain_grad: float32 [1152], P('col')
- w_qkv_grad: float32 [1152, 6, 320], P('col', 'row')
- w_out_grad: float32 [1152, 6, 192], P('col', 'row')
- w_gate_up_grad: float32 [1152, 2, 3072], P('col', None, 'row')
- w_down_grad: float32 [1152, 3072], P('col', 'row')
Inputs may be any that keep to these rules, and one draw needn't show every extreme that they name: `segment_ids`: each sequence of 4096 tokens is a run of whole documents numbered 0, 1, 2, ... in order, each of 200 to 2000 tokens, the first exactly 2000, followed by at least one padding token with segment -1. doc_starts[s, d] is the index within sequence s of the first token of its document d; slots after its last document hold 4096.
All inputs are finite; a program needn't handle non-finite values.
Results may differ from a plain program's by a relative error of at most 0.014.
Values may be sent and summed in bfloat16 or wider, within the bound.
No kernel may reach another device: no remote copies, remote signals or barrier semaphores. Data moves between devices by JAX's collectives and lax.ppermute only.
A program may use at most 192 MiB of HBM per device.

v0:
```python
import math
import jax
import jax.numpy as jnp
from jax import lax
from jax.sharding import PartitionSpec as P

QUERY_HEADS = 18
KEY_VALUE_HEADS = 6
HEAD_WIDTH = 64
SEQ_CAP = 4096
DOC_CAP = 2000
epsilon = 1e-05
rope_base = 10000.0
masked_score = -1e30


def shifted(value, axis, steps):
    count = lax.axis_size(axis)
    leading, last = (max(0, -steps), min(count, count - steps))
    return lax.ppermute(value, axis, [(source, source + steps) for source in range(leading, last)])


def rms_parts(values):
    inverse = lax.rsqrt(jnp.mean(values * values, axis=-1, keepdims=True) + epsilon)
    return (values * inverse, inverse)


def rms_back(grad_normed, normed, inverse):
    return inverse * (grad_normed - normed * jnp.mean(grad_normed * normed, axis=-1, keepdims=True))


def rope_tables(position):
    half_width = HEAD_WIDTH // 2
    frequency = jnp.power(rope_base, -2.0 * jnp.arange(half_width, dtype=jnp.float32) / HEAD_WIDTH)
    angles = position[:, None] * frequency[None, :]
    return (jnp.cos(angles), jnp.sin(angles))


def rotate_pairs(values, cosine_values, sine_values):
    half_width = values.shape[-1] // 2
    lower_half = values[..., :half_width]
    upper_half = values[..., half_width:]
    return jnp.concatenate(
        [
            lower_half * cosine_values - upper_half * sine_values,
            upper_half * cosine_values + lower_half * sine_values,
        ],
        axis=-1,
    )


def local(
    tokens,
    segment_ids,
    doc_starts,
    norm1_gain,
    norm2_gain,
    query_key_value_weight,
    output_weight,
    w_gate_up,
    w_down,
    cotangent,
):
    tok_count = tokens.shape[0]
    column = lax.axis_index("col")
    seq_len = min(SEQ_CAP, tok_count * lax.axis_size("col"))
    doc_most = min(DOC_CAP, seq_len // 2)
    back_shards = (doc_most + tok_count - 2) // tok_count
    rows_per_block = min(512, tok_count)
    block_list = tok_count // rows_per_block
    heads_local = query_key_value_weight.shape[1]
    group_width = QUERY_HEADS // KEY_VALUE_HEADS
    query_feature_width = group_width * HEAD_WIDTH
    score_scale = 1.0 / math.sqrt(HEAD_WIDTH)
    gain_one, gain_two, full_qkv, full_out, full_gate_up, full_down = (
        lax.all_gather(norm1_gain, "col", axis=0, tiled=True),
        lax.all_gather(norm2_gain, "col", axis=0, tiled=True),
        lax.all_gather(query_key_value_weight, "col", axis=0, tiled=True),
        lax.all_gather(output_weight, "col", axis=0, tiled=True),
        lax.all_gather(w_gate_up, "col", axis=0, tiled=True),
        lax.all_gather(w_down, "col", axis=0, tiled=True),
    )
    gain_one = gain_one.astype(jnp.float32)
    gain_two = gain_two.astype(jnp.float32)
    offset = column * tok_count
    global_rows = offset + jnp.arange(tok_count, dtype=jnp.int32)
    seq_index = offset // seq_len
    in_seq = global_rows - seq_index * seq_len
    chosen = jnp.arange(doc_starts.shape[0], dtype=jnp.int32) == seq_index
    start_row = jnp.sum(jnp.where(chosen[:, None], doc_starts, 0), axis=0)
    matches = segment_ids[:, None] == jnp.arange(doc_starts.shape[1], dtype=jnp.int32)[None, :]
    begins = jnp.sum(jnp.where(matches, start_row[None, :], 0), axis=1)
    begin_global = seq_index * seq_len + begins
    cosine_values, sine_values = rope_tables((in_seq - begins).astype(jnp.float32))
    layer_input = tokens.astype(jnp.float32)
    normed_one, inverse_one = rms_parts(layer_input)
    input_one = (normed_one * gain_one).astype(jnp.bfloat16)
    projected_rows = jnp.einsum(
        "td,dhe->the", input_one, full_qkv, preferred_element_type=jnp.float32
    )
    query_raw = projected_rows[..., :query_feature_width].reshape(
        tok_count, heads_local, group_width, HEAD_WIDTH
    )
    query_matrix = rotate_pairs(
        query_raw, cosine_values[:, None, None, :], sine_values[:, None, None, :]
    ).astype(jnp.bfloat16)
    key_rows = rotate_pairs(
        projected_rows[..., query_feature_width : query_feature_width + HEAD_WIDTH],
        cosine_values[:, None, :],
        sine_values[:, None, :],
    ).astype(jnp.bfloat16)
    value_rows = projected_rows[..., query_feature_width + HEAD_WIDTH :].astype(jnp.bfloat16)
    segment_float = segment_ids.astype(jnp.bfloat16)
    key_parts = [key_rows]
    value_parts = [value_rows]
    segment_parts = [segment_float]
    for distance in range(1, back_shards + 1):
        moved = shifted((key_rows, value_rows, segment_float), "col", distance)
        key_parts.insert(0, moved[0])
        value_parts.insert(0, moved[1])
        segment_parts.insert(0, moved[2])
    key_all = jnp.concatenate(key_parts, axis=0)
    value_all = jnp.concatenate(value_parts, axis=0)
    segment_all = jnp.concatenate(segment_parts, axis=0)
    key_global = offset - back_shards * tok_count + jnp.arange(key_all.shape[0], dtype=jnp.int32)
    same_seq = jnp.floor_divide(key_global, seq_len) == seq_index
    key_padding = (segment_all < 0) & same_seq
    row_blocks = global_rows.reshape(block_list, rows_per_block)
    segment_blocks = segment_float.reshape(block_list, rows_per_block)
    begin_blocks = begin_global.reshape(block_list, rows_per_block)
    query_heads = jnp.moveaxis(
        query_matrix.reshape(block_list, rows_per_block, heads_local, group_width, HEAD_WIDTH), 2, 0
    )
    key_heads = jnp.moveaxis(key_all, 1, 0)
    value_heads = jnp.moveaxis(value_all, 1, 0)

    def scores_for(query_block, head_keys, rows_block, segment_block, begin_block):
        live_query = segment_block[:, None] >= 0
        causal = key_global[None, :] <= rows_block[:, None]
        in_doc = same_seq[None, :] & (key_global[None, :] >= begin_block[:, None])
        allowed = causal & jnp.where(live_query, in_doc, key_padding[None, :])
        allowed = allowed | (key_global[None, :] == rows_block[:, None])
        scores = (
            jnp.einsum("qgd,kd->gqk", query_block, head_keys, preferred_element_type=jnp.float32)
            * score_scale
        )
        return (scores, allowed)

    def forward_head(packed):
        head_queries, head_keys, head_values = packed

        def forward_block(inner):
            query_block, rows_block, segment_block, begin_block = inner
            scores, allowed = scores_for(
                query_block, head_keys, rows_block, segment_block, begin_block
            )
            scores = jnp.where(allowed[None], scores, masked_score)
            row_peak = jnp.max(scores, axis=-1, keepdims=True)
            exponents = jnp.exp(scores - row_peak)
            denominator = jnp.sum(exponents, axis=-1, keepdims=True)
            probs_low = (exponents / denominator).astype(jnp.bfloat16)
            attended_context = jnp.einsum(
                "gqk,kd->qgd", probs_low, head_values, preferred_element_type=jnp.float32
            )
            return (attended_context, (row_peak + jnp.log(denominator))[..., 0])

        return lax.map(forward_block, (head_queries, row_blocks, segment_blocks, begin_blocks))

    contexts, log_totals = lax.map(forward_head, (query_heads, key_heads, value_heads))
    context_low = (
        jnp.moveaxis(contexts, 0, 2)
        .reshape(tok_count, heads_local, query_feature_width)
        .astype(jnp.bfloat16)
    )
    attention = lax.psum(
        jnp.einsum("the,dhe->td", context_low, full_out, preferred_element_type=jnp.float32), "row"
    )
    residual = layer_input + attention
    normed_two, inverse_two = rms_parts(residual)
    input_two = (normed_two * gain_two).astype(jnp.bfloat16)
    gate_up = jnp.einsum("td,dcf->tcf", input_two, full_gate_up, preferred_element_type=jnp.float32)
    gate_value = gate_up[:, 0]
    up_value = gate_up[:, 1]
    gate_act = jax.nn.silu(gate_value)
    hidden = (gate_act * up_value).astype(jnp.bfloat16)
    feed = lax.psum(
        jnp.einsum("tf,df->td", hidden, full_down, preferred_element_type=jnp.float32).astype(
            jnp.bfloat16
        ),
        "row",
    ).astype(jnp.float32)
    layer_output = (residual + feed).astype(jnp.bfloat16)
    back_qkv, back_out, back_gate_up, back_down = (
        lax.all_gather(query_key_value_weight, "col", axis=0, tiled=True),
        lax.all_gather(output_weight, "col", axis=0, tiled=True),
        lax.all_gather(w_gate_up, "col", axis=0, tiled=True),
        lax.all_gather(w_down, "col", axis=0, tiled=True),
    )
    live_rows = (segment_ids >= 0).astype(jnp.float32)
    grad_out = cotangent.astype(jnp.float32) * live_rows[:, None]
    grad_feed = grad_out.astype(jnp.bfloat16)
    down_grad = jnp.einsum("tf,td->df", hidden, grad_feed, preferred_element_type=jnp.float32)
    grad_hidden = jnp.einsum("td,df->tf", grad_feed, back_down, preferred_element_type=jnp.float32)
    sigmoid_gate = jax.nn.sigmoid(gate_value)
    grad_gate = grad_hidden * up_value * sigmoid_gate * (1.0 + gate_value * (1.0 - sigmoid_gate))
    grad_up = grad_hidden * gate_act
    grad_gate_up = jnp.stack([grad_gate, grad_up], axis=1).astype(jnp.bfloat16)
    gate_up_grad = jnp.einsum(
        "td,tcf->dcf", input_two, grad_gate_up, preferred_element_type=jnp.float32
    )
    grad_input_two = lax.psum(
        jnp.einsum("tcf,dcf->td", grad_gate_up, back_gate_up, preferred_element_type=jnp.float32),
        "row",
    )
    gain_two_grad = jnp.sum(grad_input_two * normed_two, axis=0)
    grad_residual = grad_out + rms_back(grad_input_two * gain_two, normed_two, inverse_two)
    grad_attention = grad_residual.astype(jnp.bfloat16)
    out_grad = jnp.einsum(
        "the,td->dhe", context_low, grad_attention, preferred_element_type=jnp.float32
    )
    grad_context = jnp.einsum(
        "td,dhe->the", grad_attention, back_out, preferred_element_type=jnp.float32
    ).astype(jnp.bfloat16)
    grad_heads = jnp.moveaxis(
        grad_context.reshape(block_list, rows_per_block, heads_local, group_width, HEAD_WIDTH), 2, 0
    )

    def backward_head(packed):
        head_queries, head_keys, head_values, head_grads, head_logs = packed

        def backward_block(carry, inner):
            key_acc, value_acc = carry
            query_block, grad_block, log_block, rows_block, segment_block, begin_block = inner
            scores, allowed = scores_for(
                query_block, head_keys, rows_block, segment_block, begin_block
            )
            probs = jnp.where(allowed[None], jnp.exp(scores - log_block[..., None]), 0.0)
            value_acc = value_acc + jnp.einsum(
                "gqk,qgd->kd",
                probs.astype(jnp.bfloat16),
                grad_block,
                preferred_element_type=jnp.float32,
            )
            grad_probs = jnp.einsum(
                "qgd,kd->gqk", grad_block, head_values, preferred_element_type=jnp.float32
            )
            inner_sum = jnp.sum(probs * grad_probs, axis=-1, keepdims=True)
            grad_scores = (probs * (grad_probs - inner_sum)).astype(jnp.bfloat16)
            grad_query = (
                jnp.einsum(
                    "gqk,kd->qgd", grad_scores, head_keys, preferred_element_type=jnp.float32
                )
                * score_scale
            )
            key_acc = (
                key_acc
                + jnp.einsum(
                    "gqk,qgd->kd", grad_scores, query_block, preferred_element_type=jnp.float32
                )
                * score_scale
            )
            return ((key_acc, value_acc), grad_query)

        zero_rows = jnp.zeros(head_keys.shape, jnp.float32)
        (key_acc, value_acc), grad_queries = lax.scan(
            backward_block,
            (zero_rows, zero_rows),
            (head_queries, head_grads, head_logs, row_blocks, segment_blocks, begin_blocks),
        )
        return (grad_queries, key_acc, value_acc)

    grad_queries, key_grads, value_grads = lax.map(
        backward_head, (query_heads, key_heads, value_heads, grad_heads, log_totals)
    )
    key_grads = jnp.moveaxis(key_grads, 0, 1)
    value_grads = jnp.moveaxis(value_grads, 0, 1)
    own_start = back_shards * tok_count
    key_own = key_grads[own_start:]
    value_own = value_grads[own_start:]
    for distance in range(1, back_shards + 1):
        first_row = (back_shards - distance) * tok_count
        returned = (
            shifted(
                key_grads[first_row : first_row + tok_count].astype(jnp.bfloat16), "col", -distance
            ).astype(jnp.float32),
            shifted(
                value_grads[first_row : first_row + tok_count].astype(jnp.bfloat16),
                "col",
                -distance,
            ).astype(jnp.float32),
        )
        key_own = key_own + returned[0]
        value_own = value_own + returned[1]
    grad_query_rows = jnp.moveaxis(grad_queries, 0, 2).reshape(
        tok_count, heads_local, group_width, HEAD_WIDTH
    )
    query_back = rotate_pairs(
        grad_query_rows, cosine_values[:, None, None, :], -sine_values[:, None, None, :]
    ).reshape(tok_count, heads_local, query_feature_width)
    key_back = rotate_pairs(key_own, cosine_values[:, None, :], -sine_values[:, None, :])
    grad_projected = jnp.concatenate([query_back, key_back, value_own], axis=-1).astype(
        jnp.bfloat16
    )
    qkv_grad = jnp.einsum(
        "td,the->dhe", input_one, grad_projected, preferred_element_type=jnp.float32
    )
    grad_input_one = lax.psum(
        jnp.einsum("the,dhe->td", grad_projected, back_qkv, preferred_element_type=jnp.float32),
        "row",
    )
    gain_one_grad = jnp.sum(grad_input_one * normed_one, axis=0)
    input_grad = grad_residual + rms_back(grad_input_one * gain_one, normed_one, inverse_one)
    share_one, share_two, share_qkv, share_out, share_gate_up, share_down = (
        lax.psum_scatter(gain_one_grad, "col", scatter_dimension=0, tiled=True),
        lax.psum_scatter(gain_two_grad, "col", scatter_dimension=0, tiled=True),
        lax.psum_scatter(qkv_grad, "col", scatter_dimension=0, tiled=True),
        lax.psum_scatter(out_grad, "col", scatter_dimension=0, tiled=True),
        lax.psum_scatter(gate_up_grad, "col", scatter_dimension=0, tiled=True),
        lax.psum_scatter(down_grad, "col", scatter_dimension=0, tiled=True),
    )
    total_one, total_two, total_qkv, total_out, total_gate_up, total_down = lax.psum(
        (share_one, share_two, share_qkv, share_out, share_gate_up, share_down), "dp"
    )
    return (
        layer_output,
        input_grad,
        total_one,
        total_two,
        total_qkv,
        total_out,
        total_gate_up,
        total_down,
    )


def solution(mesh):
    placed = (
        P(("dp", "col"), None),
        P(("dp", "col")),
        P("dp", None),
        P("col"),
        P("col"),
        P("col", "row", None),
        P("col", "row", None),
        P("col", None, "row"),
        P("col", "row"),
        P(("dp", "col"), None),
    )
    return jax.shard_map(
        local,
        mesh=mesh,
        in_specs=placed,
        out_specs=(
            P(("dp", "col"), None),
            P(("dp", "col"), None),
            P("col"),
            P("col"),
            P("col", "row", None),
            P("col", "row", None),
            P("col", None, "row"),
            P("col", "row"),
        ),
        check_vma=False,
    )
```

profile of v0, /device:TPU:0, one launch (start us, length us, event | category | flops | bytes accessed | tf_op | source)
XLA Modules:
  0.0 2066.5 jit_solution(14559142088123442937)
XLA Ops:
  8.7 6.0 collective-permute-start.4
  24.4 10.0 all-reduce.7
  35.0 33.1 %all-gather.5.cloned.1.call-done = bf16[1152,3,320]{2,0,1:T(8,128)(2,1)} async-done(((bf16[288,3,320]{2,0,1:T(8,128)(2,1)}), bf16[1152,3,320]{2,0,1:T(8,128)(2,1)}) %all-gather.5.cloned.1.call-update) | async-done | bytes 2211856 | tf_op jit(solution)/shard_map/all_gather | solution.py:78
  88.3 6.9 collective-permute-done
  95.2 16.9 collective-permute-done.1
  114.1 14.7 collective-permute-done.2
  128.8 10.1 collective-permute-done.3
  141.1 120.9 %while.68 = (s32[]{:T(128)}, bf16[3,2,512,3,64]{2,4,3,1,0:T(8,128)(2,1)}, f32[3,2,3,512]{3,2,1,0:T(4,128)}, bf16[3,2,512,3,64]{2,4,3,1,0:T(8,128)(2,1)}, bf16[3,...) while((s32[]{:T(128)}, ...), condition=%wide.region_7.8_spmd.clone.clone.clone, body=%wide.region_2.0_spmd.clone.clone.sunk.clone | while | flops 1275651072 | bytes 67578264 | solution.py:169
  143.9 36.5 %while.67 = (s32[]{:T(128)}, bf16[2,512,3,64]{1,3,2,0:T(8,128)(2,1)S(1)}, f32[2,3,512]{2,1,0:T(4,128)S(1)}, s32[3072]{0:T(1024)S(1)}, s32[2,512]{1,0:T(2,128)S(1...) while((s32[]{:T(128)}, ...), condition=%wide.region_6.6_spmd, body=%wide.region_3.5_spmd.sunk | while | flops 1275592704 | bytes 64383120 | solution.py:167
  184.0 36.5 %while.67 = (s32[]{:T(128)}, bf16[2,512,3,64]{1,3,2,0:T(8,128)(2,1)S(1)}, f32[2,3,512]{2,1,0:T(4,128)S(1)}, s32[3072]{0:T(1024)S(1)}, s32[2,512]{1,0:T(2,128)S(1...) while((s32[]{:T(128)}, ...), condition=%wide.region_6.6_spmd, body=%wide.region_3.5_spmd.sunk | while | flops 1275592704 | bytes 64383120 | solution.py:167
  224.2 36.5 %while.67 = (s32[]{:T(128)}, bf16[2,512,3,64]{1,3,2,0:T(8,128)(2,1)S(1)}, f32[2,3,512]{2,1,0:T(4,128)S(1)}, s32[3072]{0:T(1024)S(1)}, s32[2,512]{1,0:T(2,128)S(1...) while((s32[]{:T(128)}, ...), condition=%wide.region_6.6_spmd, body=%wide.region_3.5_spmd.sunk | while | flops 1275592704 | bytes 64383120 | solution.py:167
  265.6 6.0 convolution_bitcast_fusion.3
  276.0 132.3 %all-reduce.14.cloned.1.call-done = f32[1024,1152]{1,0:T(8,128)} async-done(((f32[1024,1152]{1,0:T(8,128)}), f32[1024,1152]{1,0:T(8,128)}) %all-reduce.14.cloned.1.call-update) | async-done | bytes 4718608 | tf_op jit(solution)/shard_map/psum | solution.py:175
  413.4 125.1 %all-gather.9.cloned.1.call-done = bf16[1152,2,1536]{2,0,1:T(8,128)(2,1)} async-done(((bf16[288,2,1536]{2,0,1:T(8,128)(2,1)}), bf16[1152,2,1536]{2,0,1:T(8,128)(2,1)}) %all-gather.9.cloned.1.call-update) | async-done | bytes 7077904 | tf_op jit(solution)/shard_map/all_gather | solution.py:80
  538.5 15.3 fusion.106
  553.8 54.3 %all-gather.11.cloned.1.call-done = bf16[1152,1536]{1,0:T(8,128)(2,1)} async-done(((bf16[288,1536]{1,0:T(8,128)(2,1)}), bf16[1152,1536]{1,0:T(8,128)(2,1)}) %all-gather.11.cloned.1.call-update) | async-done | bytes 3538960 | tf_op jit(solution)/shard_map/all_gather | solution.py:81
  608.1 11.8 fusion.86
  622.6 10.0 convolution_bitcast_fusion.2
  632.8 8.6 convolution_convert_fusion
  645.2 105.3 %all-reduce.18.cloned.1.call-done = f32[1024,1152]{1,0:T(8,128)} async-done(((f32[1024,1152]{1,0:T(8,128)}), f32[1024,1152]{1,0:T(8,128)}) %all-reduce.18.cloned.1.call-update) | async-done | bytes 4718608 | tf_op jit(solution)/shard_map/psum | solution.py:211
  756.6 65.5 %all-reduce.16.cloned.1.call-done = bf16[1024,1152]{1,0:T(8,128)(2,1)} async-done(((bf16[1024,1152]{1,0:T(8,128)(2,1)}), bf16[1024,1152]{1,0:T(8,128)(2,1)}) %all-reduce.16.cloned.1.call-update) | async-done | bytes 2359312 | tf_op jit(solution)/shard_map/psum | solution.py:186
  822.2 6.4 multiply_add_fusion
  841.4 418.1 %while.70 = (s32[]{:T(128)}, f32[3,2,512,3,64]{2,4,3,1,0:T(8,128)}, f32[3,3072,64]{1,2,0:T(8,128)}, f32[3,3072,64]{1,2,0:T(8,128)}, bf16[3,2,512,3,64]{2,4,3,1,0...) while((s32[]{:T(128)}, f32[3,2,512,3,64]{2,4,3,1,0:T(8,128)}, ...), condition=%wide.region_17.18_spmd.clone.clone.clone, body=%wide.region_13.17_spmd.clone.clone.sunk.clone | while | flops 3102827520 | bytes 211725008 | solution.py:272
  849.8 128.0 %while.69 = (s32[]{:T(128)}, f32[3072,64]{0,1:T(8,128)S(1)}, f32[3072,64]{0,1:T(8,128)}, f32[2,512,3,64]{1,3,2,0:T(8,128)}, s32[3072]{0:T(1024)}, /*index=5*/s32...) while((s32[]{:T(128)}, f32[3072,64]{0,1:T(8,128)S(1)}, ...), condition=%wide.region_16.16_spmd.clone, body=%wide.region_14.15_spmd.clone.sunk | while | flops 3102769152 | bytes 200669552 | solution.py:265
  854.4 8.1 fusion.167
  862.5 13.4 fusion.168
  875.9 18.0 fusion.169
  904.4 9.6 fusion.171
  918.5 8.0 fusion.167
  926.5 13.3 fusion.168
  939.9 17.9 fusion.169
  968.1 9.7 fusion.171
  989.3 127.6 %while.69 = (s32[]{:T(128)}, f32[3072,64]{0,1:T(8,128)S(1)}, f32[3072,64]{0,1:T(8,128)}, f32[2,512,3,64]{1,3,2,0:T(8,128)}, s32[3072]{0:T(1024)}, /*index=5*/s32...) while((s32[]{:T(128)}, f32[3072,64]{0,1:T(8,128)S(1)}, ...), condition=%wide.region_16.16_spmd.clone, body=%wide.region_14.15_spmd.clone.sunk | while | flops 3102769152 | bytes 200669552 | solution.py:265
  993.8 8.0 fusion.167
  1001.8 13.3 fusion.168
  1015.2 17.9 fusion.169
  1043.4 9.5 fusion.171
  1057.5 8.0 fusion.167
  1065.5 13.4 fusion.168
  1078.9 17.9 fusion.169
  1107.1 9.7 fusion.171
  1128.3 127.6 %while.69 = (s32[]{:T(128)}, f32[3072,64]{0,1:T(8,128)S(1)}, f32[3072,64]{0,1:T(8,128)}, f32[2,512,3,64]{1,3,2,0:T(8,128)}, s32[3072]{0:T(1024)}, /*index=5*/s32...) while((s32[]{:T(128)}, f32[3072,64]{0,1:T(8,128)S(1)}, ...), condition=%wide.region_16.16_spmd.clone, body=%wide.region_14.15_spmd.clone.sunk | while | flops 3102769152 | bytes 200669552 | solution.py:265
  1132.8 8.0 fusion.167
  1140.8 13.3 fusion.168
  1154.2 17.9 fusion.169
  1182.4 9.5 fusion.171
  1196.5 8.0 fusion.167
  1204.5 13.4 fusion.168
  1217.9 17.9 fusion.169
  1246.1 9.7 fusion.171
  1268.8 8.9 collective-permute-done.6
  1277.7 25.3 %collective-permute-done.7 = bf16[1024,3,64]{0,2,1:T(8,128)(2,1)S(1)} collective-permute-done((bf16[1024,3,64]{0,2,1:T(8,128)(2,1)S(1)}, bf16[1024,3,64]{0,2,1:T(8,128)(2,1)S(1)}, u32[]{:S(2)}, u32[]{:S(2)}) %collective-permute-start.7) | collective-permute-done | bytes 393248 | tf_op jit(solution)/shard_map/ppermute | solution.py:20
  1303.3 15.3 collective-permute-done.9
  1326.1 9.4 fusion.98
  1336.3 14.5 fusion.84
  1350.8 7.9 convolution_bitcast_fusion.1
  1358.9 58.9 %reduce-scatter.5.cloned.1.call-done = f32[288,3,320]{2,0,1:T(8,128)} async-done(((f32[1152,3,320]{2,0,1:T(8,128)}), f32[288,3,320]{2,0,1:T(8,128)}) %reduce-scatter.5.cloned.1.call-update) | async-done | bytes 1105936 | tf_op jit(solution)/shard_map/reduce_scatter | solution.py:316
  1417.7 126.2 %reduce-scatter.11.cloned.1.call-done = f32[288,1536]{1,0:T(8,128)} async-done(((f32[1152,1536]{1,0:T(8,128)}), f32[288,1536]{1,0:T(8,128)}) %reduce-scatter.11.cloned.1.call-update) | async-done | bytes 1769488 | tf_op jit(solution)/shard_map/reduce_scatter | solution.py:319
  1543.9 240.2 %reduce-scatter.9.cloned.1.call-done = f32[288,2,1536]{2,0,1:T(8,128)} async-done(((f32[1152,2,1536]{2,0,1:T(8,128)}), f32[288,2,1536]{2,0,1:T(8,128)}) %reduce-scatter.9.cloned.1.call-update) | async-done | bytes 3538960 | tf_op jit(solution)/shard_map/reduce_scatter | solution.py:318
  1784.8 122.5 %all-reduce.20.cloned.1.call-done = f32[1024,1152]{1,0:T(8,128)} async-done(((f32[1024,1152]{1,0:T(8,128)}), f32[1024,1152]{1,0:T(8,128)}) %all-reduce.20.cloned.1.call-update) | async-done | bytes 4718608 | tf_op jit(solution)/shard_map/psum | solution.py:307
  1910.8 18.7 all-reduce.4
  1929.7 7.3 all-reduce.5
  1942.8 107.0 %all-reduce.22.cloned.1.call-done = (f32[288,3,320]{2,0,1:T(8,128)}, f32[288,3,192]{2,0,1:T(8,128)}, f32[288,2,1536]{2,0,1:T(8,128)}, f32[288,1536]{1,0:T(8,128)}) async-done(((f32[288,3,320]{2,0,1:T(8,128)}, f32[288,3,192]{2,0,1:T(8,128)}, f32[288,2,1536]{2,0,1:T(8,128)}, f32[288,1536]{1,0:T(8,128)}), (f32[288,3,320]{2,0,1:T(8,128)}, f32[288,3,192]{2,0,1:T(8,128)}, f32[288,2,1536]{2,0,1:T(8,128)}, ...) | async-done | bytes 7077904 | tf_op jit(solution)/shard_map/psum | solution.py:321
  2049.8 6.7 copy.57
  (403 shorter events, 348.1 us)
Async XLA Ops:
  7.2 15.5 copy-start.40
  7.2 13.7 copy-start.3
  7.2 16.7 copy-start.41
  7.2 16.9 copy-start.42
  7.2 60.9 %all-gather.5.cloned.1.call-start = ((), (), s32[]{:S(2)}) async-start(), calls=%async_computation.4 | async-start | bytes 3317760 | tf_op jit(solution)/shard_map/all_gather | solution.py:78
  7.9 257.6 %all-gather.7.cloned.1.call-start = ((), (), s32[]{:S(2)}) async-start(), calls=%async_computation.5 | async-start | bytes 2211840 | tf_op jit(solution)/shard_map/all_gather | solution.py:79
  8.7 26.3 %collective-permute-start.4 = (bf16[1024]{0:T(1024)(128)(2,1)S(1)}, bf16[1024]{0:T(1024)(128)(2,1)S(1)}, u32[]{:S(2)}, u32[]{:S(2)}) collective-permute-start(bf16[1024]{0:T(1024)(128)(2,1)S(1)} %convert_element_type.96), channel_id=1, source_target_pairs={{0,2},{1,3},{4,6},{5,7},{8,10},{9,11},{12,14},{13,15},{16,18},{17,... | collective-permute-start | bytes 6152 | tf_op jit(solution)/shard_map/ppermute | solution.py:20
  14.6 20.3 collective-permute-start.5
  18.2 390.1 %all-reduce.14.cloned.1.call-start = ((), (), s32[]{:S(2)}) async-start(), calls=%async_computation.6 | async-start | bytes 9437184 | tf_op jit(solution)/shard_map/psum | solution.py:175
  21.4 51.5 %copy-start.33 = (f32[1024]{0:T(1024)}, f32[1024]{0:T(1024)S(1)}, u32[]{:S(2)}) copy-start(f32[1024]{0:T(1024)S(1)} %add_rsqrt_fusion.1) | copy-start | bytes 12292
  22.6 50.3 %copy-start.23 = (f32[1024,32]{0,1:T(8,128)}, f32[1024,32]{0,1:T(8,128)S(1)}, u32[]{:S(2)}) copy-start(f32[1024,32]{0,1:T(8,128)S(1)} %get-tuple-element.777) | copy-start | bytes 393220
  22.6 61.6 %copy-start.13 = (f32[1024,32]{0,1:T(8,128)}, f32[1024,32]{0,1:T(8,128)S(1)}, u32[]{:S(2)}) copy-start(f32[1024,32]{0,1:T(8,128)S(1)} %get-tuple-element.778) | copy-start | bytes 393220
  34.4 38.5 %copy-start.30 = (f32[1152]{0:T(1024)}, f32[1152]{0:T(1024)S(1)}, u32[]{:S(2)}) copy-start(f32[1152]{0:T(1024)S(1)} %convert_element_type.93) | copy-start | bytes 13828
  73.0 11.2 copy-start.24
  73.8 21.4 %collective-permute-start = (bf16[1024,3,64]{0,2,1:T(8,128)(2,1)}, bf16[1024,3,64]{0,2,1:T(8,128)(2,1)S(1)}, u32[]{:S(2)}, u32[]{:S(2)}) collective-permute-start(bf16[1024,3,64]{0,2,1:T(8,128)(2,1)} %pad_maximum_fusion.5), channel_id=1, source_target_pairs={{0,2},{1,3},{4,6},{5,7},{8,10},{9,11},{12,14},{13,15},{16,18},{17,... | collective-permute-start | bytes 1179656 | tf_op jit(solution)/shard_map/ppermute | solution.py:20
  77.0 35.1 %collective-permute-start.1 = (bf16[1024,3,64]{0,2,1:T(8,128)(2,1)}, bf16[1024,3,64]{0,2,1:T(8,128)(2,1)}, u32[]{:S(2)}, u32[]{:S(2)}) collective-permute-start(bf16[1024,3,64]{0,2,1:T(8,128)(2,1)} %pad_maximum_fusion.5), channel_id=1, source_target_pairs={{0,1},{1,2},{2,3},{4,5},{5,6},{6,7},{8,9},{9,10},{10,11},{12,13},{... | collective-permute-start | bytes 1179656 | tf_op jit(solution)/shard_map/ppermute | solution.py:20
  80.1 48.6 %collective-permute-start.2 = (bf16[1024,3,64]{0,2,1:T(8,128)(2,1)S(1)}, bf16[1024,3,64]{0,2,1:T(8,128)(2,1)}, u32[]{:S(2)}, u32[]{:S(2)}) collective-permute-start(bf16[1024,3,64]{0,2,1:T(8,128)(2,1)S(1)} %slice.141), channel_id=1, source_target_pairs={{0,2},{1,3},{4,6},{5,7},{8,10},{9,11},{12,14},{13,15},{16,18},{17,... | collective-permute-start | bytes 1179656 | tf_op jit(solution)/shard_map/ppermute | solution.py:20
  82.2 56.7 %collective-permute-start.3 = (bf16[1024,3,64]{0,2,1:T(8,128)(2,1)S(1)}, bf16[1024,3,64]{0,2,1:T(8,128)(2,1)}, u32[]{:S(2)}, u32[]{:S(2)}) collective-permute-start(bf16[1024,3,64]{0,2,1:T(8,128)(2,1)S(1)} %slice.141), channel_id=1, source_target_pairs={{0,1},{1,2},{2,3},{4,5},{5,6},{6,7},{8,9},{9,10},{10,11},{12,13},{... | collective-permute-start | bytes 1179656 | tf_op jit(solution)/shard_map/ppermute | solution.py:20
  271.6 136.7 %copy-start.4 = (bf16[1024,1152]{1,0:T(8,128)(2,1)S(1)}, bf16[1024,1152]{1,0:T(8,128)(2,1)}, u32[]{:S(2)}) copy-start(bf16[1024,1152]{1,0:T(8,128)(2,1)} %param.18) | copy-start | bytes 7077892
  271.6 266.9 %all-gather.9.cloned.1.call-start = ((), (), s32[]{:S(2)}) async-start(), calls=%async_computation.7 | async-start | bytes 8847360 | tf_op jit(solution)/shard_map/all_gather | solution.py:80
  274.7 333.4 %all-gather.11.cloned.1.call-start = ((), (), s32[]{:S(2)}) async-start(), calls=%async_computation.8 | async-start | bytes 4423680 | tf_op jit(solution)/shard_map/all_gather | solution.py:81
  275.3 475.3 %all-reduce.18.cloned.1.call-start = ((), (), s32[]{:S(2)}) async-start(), calls=%async_computation.10 | async-start | bytes 9437184 | tf_op jit(solution)/shard_map/psum | solution.py:211
  276.0 546.2 %copy-start.37 = (f32[1024]{0:T(1024)}, f32[1024]{0:T(1024)S(1)}, u32[]{:S(2)}) copy-start(f32[1024]{0:T(1024)S(1)} %compare_convert_fusion) | copy-start | bytes 12292
  413.4 408.7 %copy-start.19 = (f32[1024]{0:T(1024)}, f32[1024]{0:T(1024)S(1)}, u32[]{:S(2)}) copy-start(f32[1024]{0:T(1024)S(1)} %add_rsqrt_fusion) | copy-start | bytes 12292
  538.5 69.6 %copy-start.17 = (bf16[1024,1152]{1,0:T(8,128)(2,1)S(1)}, bf16[1024,1152]{1,0:T(8,128)(2,1)}, u32[]{:S(2)}) copy-start(bf16[1024,1152]{1,0:T(8,128)(2,1)} %param.27) | copy-start | bytes 7077892
  608.1 14.5 copy-start.43
  632.6 189.6 %all-reduce.16.cloned.1.call-start = ((), (), s32[]{:S(2)}) async-start(), calls=%async_computation.9 | async-start | bytes 4718592 | tf_op jit(solution)/shard_map/psum | solution.py:186
  641.5 717.4 %reduce-scatter.7.cloned.1.call-start = ((), (), s32[]{:S(2)}) async-start(), calls=%async_computation.13 | async-start | bytes 4423680 | tf_op jit(solution)/shard_map/reduce_scatter | solution.py:317
  841.3 576.4 %reduce-scatter.5.cloned.1.call-start = ((), (), s32[]{:S(2)}) async-start(), calls=%async_computation.12 | async-start | bytes 6635520 | tf_op jit(solution)/shard_map/reduce_scatter | solution.py:316
  854.3 8.1 copy-start.10
  854.4 8.1 copy-start.1
  893.9 6.6 copy-start.6
  918.5 8.0 copy-start.10
  918.5 8.0 copy-start.1
  957.7 6.5 copy-start.6
  993.8 8.0 copy-start.10
  993.8 8.0 copy-start.1
  1033.1 6.5 copy-start.6
  1057.5 8.0 copy-start.10
  1057.5 8.0 copy-start.1
  1096.8 6.5 copy-start.6
  1132.8 8.0 copy-start.10
  1132.8 8.0 copy-start.1
  1172.1 6.5 copy-start.6
  1196.5 8.0 copy-start.10
  1196.5 8.0 copy-start.1
  1235.8 6.5 copy-start.6
  1263.0 14.7 collective-permute-start.6
  1264.3 38.7 %collective-permute-start.7 = (bf16[1024,3,64]{0,2,1:T(8,128)(2,1)S(1)}, bf16[1024,3,64]{0,2,1:T(8,128)(2,1)S(1)}, u32[]{:S(2)}, u32[]{:S(2)}) collective-permute-start(bf16[1024,3,64]{0,2,1:T(8,128)(2,1)S(1)} %get-tuple-element.771), channel_id=1, source_target_pairs={{2,0},{3,1},{6,4},{7,5},{10,8},{11,9},{14,12},{15,13},{18,16},{19,... | collective-permute-start | bytes 1179656 | tf_op jit(solution)/shard_map/ppermute | solution.py:20
  1265.6 37.7 %collective-permute-start.8 = (bf16[1024,3,64]{0,2,1:T(8,128)(2,1)S(1)}, bf16[1024,3,64]{0,2,1:T(8,128)(2,1)S(1)}, u32[]{:S(2)}, u32[]{:S(2)}) collective-permute-start(bf16[1024,3,64]{0,2,1:T(8,128)(2,1)S(1)} %get-tuple-element.772), channel_id=1, source_target_pairs={{1,0},{2,1},{3,2},{5,4},{6,5},{7,6},{9,8},{10,9},{11,10},{13,12},{... | collective-permute-start | bytes 1179656 | tf_op jit(solution)/shard_map/ppermute | solution.py:20
  1266.9 51.7 %collective-permute-start.9 = (bf16[1024,3,64]{0,2,1:T(8,128)(2,1)S(1)}, bf16[1024,3,64]{0,2,1:T(8,128)(2,1)S(1)}, u32[]{:S(2)}, u32[]{:S(2)}) collective-permute-start(bf16[1024,3,64]{0,2,1:T(8,128)(2,1)S(1)} %get-tuple-element.773), channel_id=1, source_target_pairs={{2,0},{3,1},{6,4},{7,5},{10,8},{11,9},{14,12},{15,13},{18,16},{19,... | collective-permute-start | bytes 1179656 | tf_op jit(solution)/shard_map/ppermute | solution.py:20
  1268.6 50.9 %copy-start.5 = (bf16[1024,1152]{1,0:T(8,128)(2,1)S(1)}, bf16[1024,1152]{1,0:T(8,128)(2,1)}, u32[]{:S(2)}) copy-start(bf16[1024,1152]{1,0:T(8,128)(2,1)} %param.18) | copy-start | bytes 7077892
  1268.7 50.9 %copy-start.31 = (f32[1152]{0:T(1024)S(1)}, f32[1152]{0:T(1024)}, u32[]{:S(2)}) copy-start(f32[1152]{0:T(1024)} %copy-done.30) | copy-start | bytes 13828
  1268.7 50.9 %copy-start.34 = (f32[1024]{0:T(1024)S(1)}, f32[1024]{0:T(1024)}, u32[]{:S(2)}) copy-start(f32[1024]{0:T(1024)} %copy-done.33) | copy-start | bytes 12292
  1303.3 15.5 copy-start.28
  1303.3 15.5 copy-start.29
  1325.5 218.5 %reduce-scatter.11.cloned.1.call-start = ((), (), s32[]{:S(2)}) async-start(), calls=%async_computation.15 | async-start | bytes 8847360 | tf_op jit(solution)/shard_map/reduce_scatter | solution.py:319
  1335.6 448.5 %reduce-scatter.9.cloned.1.call-start = ((), (), s32[]{:S(2)}) async-start(), calls=%async_computation.14 | async-start | bytes 17694720 | tf_op jit(solution)/shard_map/reduce_scatter | solution.py:318
  1350.8 556.5 %all-reduce.20.cloned.1.call-start = ((), (), s32[]{:S(2)}) async-start(), calls=%async_computation.11 | async-start | bytes 9437184 | tf_op jit(solution)/shard_map/psum | solution.py:307
  1358.8 691.1 %all-reduce.22.cloned.1.call-start = ((), (), s32[]{:S(2)}) async-start(), calls=%async_computation.16 | async-start | bytes 15040512 | tf_op jit(solution)/shard_map/psum | solution.py:321
  1784.1 123.2 %copy-start.32 = (f32[1152]{0:T(1024)S(1)}, f32[1152]{0:T(1024)}, u32[]{:S(2)}) copy-start(f32[1152]{0:T(1024)} %copy-done.30) | copy-start | bytes 13828
  1784.8 126.1 %copy-start.36 = (f32[1152]{0:T(1024)S(1)}, f32[1152]{0:T(1024)}, u32[]{:S(2)}) copy-start(f32[1152]{0:T(1024)} %get-tuple-element.623) | copy-start | bytes 13828
  2049.8 6.7 copy-start.21
  2049.8 7.7 copy-start.26
  (35 other events, 110.4 us)
Sparse Core Ops, SparseCore 0:
  9.6 58.4 all-gather.4
  69.7 63.5 all-gather.6
  271.7 136.5 all-reduce.13
  410.3 128.1 all-gather.8
  539.9 68.1 all-gather.10
  632.7 117.8 all-reduce.17
  753.4 68.6 all-reduce.15
  841.5 66.4 reduce-scatter.6
  1325.6 92.0 reduce-scatter.4
  1419.9 124.0 reduce-scatter.10
  1546.3 237.7 reduce-scatter.8
  1787.0 120.2 all-reduce.19
  1909.9 139.9 all-reduce.21
where the time goes:
time: 2080 us; the launch traced here: 2070 us
  waiting for transfers between devices  1270 us (61%)
  matrix products  396 us (19%)
  other arithmetic  226 us (11%)
  local copies, waits for them, and re-layouts  95 us (5%)
  blocking collectives  36 us (2%)
  starting transfers between devices  25.4 us (1%)
    reduce_scatter x1, waiting for transfers between devices, local(): lax.psum_scatter(gate_up_grad, 'col', scatter_dimension=0, tiled=True)  240 us
    psum x1, waiting for transfers between devices, local(): lax.psum(jnp.einsum('the,dhe->td', context_low, full_out, preferred_eleme...  132 us
    reduce_scatter x1, waiting for transfers between devices, local(): lax.psum_scatter(down_grad, 'col', scatter_dimension=0, tiled=True)  126 us
    all_gather x1, waiting for transfers between devices, local(): lax.all_gather(w_gate_up, 'col', axis=0, tiled=True)  125 us
    psum x1, waiting for transfers between devices, local(): lax.psum(jnp.einsum('the,dhe->td', grad_projected, back_qkv, preferred_el...  122 us
    convert_element_type x6, other arithmetic, backward_block(): grad_scores = (probs * (grad_probs - inner_sum)).astype(jnp.bfloat16)  107 us
    psum x1, waiting for transfers between devices, local(): lax.psum((share_one, share_two, share_qkv, share_out, share_gate_up, shar...  107 us
    psum x1, waiting for transfers between devices, local(): lax.psum(jnp.einsum('tcf,dcf->td', grad_gate_up, back_gate_up, preferred_...  105 us
  transfers between devices with their start and end apart: 23, of which 18 were waited for; matrix products, arithmetic and copies ran while one was open for 31% of the time, Pallas kernels for 0%

commit v1 on v0

--- a/solution.py
+++ b/solution.py
@@ -12,6 +12,28 @@
 epsilon = 1e-05
 rope_base = 10000.0
 masked_score = -1e30
+
+
+def joined_along(pieces, dim):
+    shape = list(pieces.shape[1:])
+    shape[dim] *= pieces.shape[0]
+    return jnp.moveaxis(pieces, 0, dim).reshape(shape)
+
+
+def collect(x, axis, dim):
+    size = lax.axis_size(axis)
+    pairs = [(i, (i + 1) % size) for i in range(size)]
+    back = [(b, a) for a, b in pairs]
+    lower, upper = ([], [])
+    for step in range(size - 1):
+        if step % 2 == 0:
+            lower.append(lax.ppermute(lower[-1] if lower else x, axis, pairs))
+        else:
+            upper.append(lax.ppermute(upper[-1] if upper else x, axis, back))
+    blocks = jnp.stack([*lower[::-1], x, *upper])
+    shift = lax.axis_index(axis) - len(lower)
+    blocks = blocks[(jnp.arange(size) - shift) % size]
+    return joined_along(blocks, dim)
 
 
 def shifted(value, axis, steps):
@@ -78,7 +100,7 @@
         lax.all_gather(query_key_value_weight, "col", axis=0, tiled=True),
         lax.all_gather(output_weight, "col", axis=0, tiled=True),
         lax.all_gather(w_gate_up, "col", axis=0, tiled=True),
-        lax.all_gather(w_down, "col", axis=0, tiled=True),
+        collect(w_down, "col", 0),
     )
     gain_one = gain_one.astype(jnp.float32)
     gain_two = gain_two.astype(jnp.float32)

time: 2080 us -> 1970 us (0.947)
  matrix products: 396 us -> 316 us
  other arithmetic: 226 us -> 197 us
    psum x1, waiting for transfers between devices: 105 us -> 33.6 us  [local(): lax.psum(jnp.einsum('tcf,dcf->td', grad_gate_up, back_gate_up, preferred_...]
    ppermute x0 -> x3, waiting for transfers between devices: none -> 56.5 us  [the longest x2 41.3 us: collect(): lower.append(lax.ppermute(lower[-1] if lower else x, axis, pairs))]
    dot_general x6, matrix products: 57.8 us -> 25.4 us  [backward_block(): jnp.einsum('gqk,qgd->kd', probs.astype(jnp.bfloat16), grad_block, preferr...]
    dot_general x12, matrix products: 69.6 us -> 37.5 us  [scores_for(): jnp.einsum('qgd,kd->gqk', query_block, head_keys, preferred_element_type=...]
    while x78 -> x36, local copies, waits for them, and re-layouts: 10.4 us -> 38.9 us
    convert_element_type x6, other arithmetic: 107 us -> 83.6 us  [backward_block(): grad_scores = (probs * (grad_probs - inner_sum)).astype(jnp.bfloat16)]
    dot_general x6, matrix products: 33.9 us -> 11.2 us  [backward_block(): jnp.einsum('gqk,qgd->kd', grad_scores, query_block, preferred_element_typ...]
  transfers between devices with their start and end apart: 23 -> 26, of which waited for: 18 -> 20; matrix products, arithmetic and copies ran while one was open for 31% -> 27% of each run, Pallas kernels for 0% -> 0%
where the time goes in v1:
time: 1970 us; the launch traced here: 1960 us
  waiting for transfers between devices  1250 us (63%)
  matrix products  316 us (16%)
  other arithmetic  197 us (10%)
  local copies, waits for them, and re-layouts  115 us (6%)
  blocking collectives  35.9 us (2%)
  starting transfers between devices  28.7 us (1%)
    reduce_scatter x1, waiting for transfers between devices, local(): lax.psum_scatter(gate_up_grad, 'col', scatter_dimension=0, tiled=True)  240 us
    psum x1, waiting for transfers between devices, local(): lax.psum(jnp.einsum('the,dhe->td', context_low, full_out, preferred_eleme...  135 us
    reduce_scatter x1, waiting for transfers between devices, local(): lax.psum_scatter(down_grad, 'col', scatter_dimension=0, tiled=True)  126 us
    all_gather x1, waiting for transfers between devices, local(): lax.all_gather(w_gate_up, 'col', axis=0, tiled=True)  125 us
    psum x1, waiting for transfers between devices, local(): lax.psum(jnp.einsum('the,dhe->td', grad_projected, back_qkv, preferred_el...  123 us
    psum x1, waiting for transfers between devices, local(): lax.psum((share_one, share_two, share_qkv, share_out, share_gate_up, shar...  107 us
    ppermute x10, waiting for transfers between devices, shifted(): lax.ppermute(value, axis, [(source, source + steps) for source in range(l...  96.8 us
    convert_element_type x6, other arithmetic, backward_block(): grad_scores = (probs * (grad_probs - inner_sum)).astype(jnp.bfloat16)  83.6 us
  transfers between devices with their start and end apart: 26, of which 20 were waited for; matrix products, arithmetic and copies ran while one was open for 27% of the time, Pallas kernels for 0%

profile of v1, /device:TPU:0, one launch (start us, length us, event | category | flops | bytes accessed | tf_op | source)
XLA Modules:
  0.0 1963.4 jit_solution(5131999138605579838)
XLA Ops:
  24.4 10.0 all-reduce.7
  34.4 33.7 %all-gather.5.cloned.1.call-done = bf16[1152,3,320]{2,0,1:T(8,128)(2,1)} async-done(((bf16[288,3,320]{2,0,1:T(8,128)(2,1)}), bf16[1152,3,320]{2,0,1:T(8,128)(2,1)}) %all-gather.5.cloned.1.call-update) | async-done | bytes 2211856 | tf_op jit(solution)/shard_map/all_gather | solution.py:100
  93.8 16.9 collective-permute-done
  112.7 14.6 collective-permute-done.3
  127.4 10.5 collective-permute-done.2
  139.9 116.6 %while.68 = (s32[]{:T(128)}, bf16[3,2,512,3,64]{2,4,3,1,0:T(8,128)(2,1)}, f32[3,2,3,512]{3,2,1,0:T(4,128)}, bf16[3,2,512,3,64]{2,4,3,1,0:T(8,128)(2,1)}, bf16[3,...) while((s32[]{:T(128)}, ...), condition=%wide.region_7.8_spmd.clone.clone.clone, body=%wide.region_2.7_spmd.clone.clone.sunk.clone | while | flops 1275651072 | bytes 67577272 | solution.py:191
  142.4 35.2 %while.67 = (s32[]{:T(128)}, bf16[2,512,3,64]{1,3,2,0:T(8,128)(2,1)S(1)}, f32[2,3,512]{2,1,0:T(4,128)S(1)}, s32[3072]{0:T(1024)S(1)}, s32[2,512]{1,0:T(2,128)S(1...) while((s32[]{:T(128)}, ...), condition=%wide.region_6.6_spmd, body=%wide.region_3.5_spmd.sunk | while | flops 1275592704 | bytes 64383128 | solution.py:189
  154.2 5.7 fusion.186
  181.2 35.2 %while.67 = (s32[]{:T(128)}, bf16[2,512,3,64]{1,3,2,0:T(8,128)(2,1)S(1)}, f32[2,3,512]{2,1,0:T(4,128)S(1)}, s32[3072]{0:T(1024)S(1)}, s32[2,512]{1,0:T(2,128)S(1...) while((s32[]{:T(128)}, ...), condition=%wide.region_6.6_spmd, body=%wide.region_3.5_spmd.sunk | while | flops 1275592704 | bytes 64383128 | solution.py:189
  193.1 5.7 fusion.186
  210.7 5.7 fusion.186
  220.0 35.2 %while.67 = (s32[]{:T(128)}, bf16[2,512,3,64]{1,3,2,0:T(8,128)(2,1)S(1)}, f32[2,3,512]{2,1,0:T(4,128)S(1)}, s32[3072]{0:T(1024)S(1)}, s32[2,512]{1,0:T(2,128)S(1...) while((s32[]{:T(128)}, ...), condition=%wide.region_6.6_spmd, body=%wide.region_3.5_spmd.sunk | while | flops 1275592704 | bytes 64383128 | solution.py:189
  231.9 5.7 fusion.186
  260.2 6.4 convolution_bitcast_fusion.3
  270.4 135.1 %all-reduce.14.cloned.1.call-done = f32[1024,1152]{1,0:T(8,128)} async-done(((f32[1024,1152]{1,0:T(8,128)}), f32[1024,1152]{1,0:T(8,128)}) %all-reduce.14.cloned.1.call-update) | async-done | bytes 4718608 | tf_op jit(solution)/shard_map/psum | solution.py:197
  410.6 125.1 %all-gather.9.cloned.1.call-done = bf16[1152,2,1536]{2,0,1:T(8,128)(2,1)} async-done(((bf16[288,2,1536]{2,0,1:T(8,128)(2,1)}), bf16[1152,2,1536]{2,0,1:T(8,128)(2,1)}) %all-gather.9.cloned.1.call-update) | async-done | bytes 7077904 | tf_op jit(solution)/shard_map/all_gather | solution.py:102
  535.7 15.2 fusion.115
  550.9 54.4 %all-gather.11.cloned.1.call-done = bf16[1152,1536]{1,0:T(8,128)(2,1)} async-done(((bf16[288,1536]{1,0:T(8,128)(2,1)}), bf16[1152,1536]{1,0:T(8,128)(2,1)}) %all-gather.11.cloned.1.call-update) | async-done | bytes 3538960 | tf_op jit(solution)/shard_map/all_gather | solution.py:219
  605.3 10.2 fusion.96
  618.1 10.0 convolution_bitcast_fusion.2
  633.1 20.5 %collective-permute-done.6 = bf16[288,1536]{1,0:T(8,128)(2,1)S(1)} collective-permute-done((bf16[288,1536]{1,0:T(8,128)(2,1)S(1)}, bf16[288,1536]{1,0:T(8,128)(2,1)S(1)}, u32[]{:S(2)}, u32[]{:S(2)}) %collective-permute-start.6) | collective-permute-done | bytes 884768 | tf_op jit(solution)/shard_map/ppermute | solution.py:30
  654.3 15.2 collective-permute-done.8
  669.4 20.8 %collective-permute-done.7 = bf16[288,1536]{1,0:T(8,128)(2,1)S(1)} collective-permute-done((bf16[288,1536]{1,0:T(8,128)(2,1)S(1)}, bf16[288,1536]{1,0:T(8,128)(2,1)S(1)}, u32[]{:S(2)}, u32[]{:S(2)}) %collective-permute-start.7) | collective-permute-done | bytes 884768 | tf_op jit(solution)/shard_map/ppermute | solution.py:30
  696.8 12.1 convolution_convert_fusion
  712.5 33.6 %all-reduce.18.cloned.1.call-done = f32[1024,1152]{1,0:T(8,128)} async-done(((f32[1024,1152]{1,0:T(8,128)}), f32[1024,1152]{1,0:T(8,128)}) %all-reduce.18.cloned.1.call-update) | async-done | bytes 4718608 | tf_op jit(solution)/shard_map/psum | solution.py:233
  752.2 65.5 %all-reduce.16.cloned.1.call-done = bf16[1024,1152]{1,0:T(8,128)(2,1)} async-done(((bf16[1024,1152]{1,0:T(8,128)(2,1)}), bf16[1024,1152]{1,0:T(8,128)(2,1)}) %all-reduce.16.cloned.1.call-update) | async-done | bytes 2359312 | tf_op jit(solution)/shard_map/psum | solution.py:208
  817.7 6.4 multiply_add_fusion
  837.0 319.0 %while.70 = (s32[]{:T(128)}, f32[3,2,512,3,64]{2,4,3,1,0:T(8,128)}, f32[3,3072,64]{1,2,0:T(8,128)}, f32[3,3072,64]{1,2,0:T(8,128)}, bf16[3,2,512,3,64]{2,4,3,1,0...) while((s32[]{:T(128)}, f32[3,2,512,3,64]{2,4,3,1,0:T(8,128)}, ...), condition=%wide.region_17.18_spmd.clone.clone.clone, body=%wide.region_13.17_spmd.clone.clone.sunk.clone | while | flops 3102827520 | bytes 243132016 | solution.py:294
  842.1 98.1 %while.69 = (s32[]{:T(128)}, f32[3072,64]{0,1:T(8,128)S(1)}, f32[3072,64]{0,1:T(8,128)}, f32[2,512,3,64]{1,3,2,0:T(8,128)S(1)}, s32[3072]{0:T(1024)S(1)}, /*inde...) while((s32[]{:T(128)}, f32[3072,64]{0,1:T(8,128)S(1)}, ...), condition=%wide.region_16.16_spmd.clone, body=%wide.region_14.15_spmd.clone.sunk | while | flops 3102769152 | bytes 235223312 | solution.py:287
  847.9 6.5 copy-done
  858.6 13.7 fusion.179
  872.4 14.0 fusion.180
  897.1 6.5 copy-done
  907.8 13.6 fusion.179
  921.4 13.9 fusion.180
  948.4 97.9 %while.69 = (s32[]{:T(128)}, f32[3072,64]{0,1:T(8,128)S(1)}, f32[3072,64]{0,1:T(8,128)}, f32[2,512,3,64]{1,3,2,0:T(8,128)S(1)}, s32[3072]{0:T(1024)S(1)}, /*inde...) while((s32[]{:T(128)}, f32[3072,64]{0,1:T(8,128)S(1)}, ...), condition=%wide.region_16.16_spmd.clone, body=%wide.region_14.15_spmd.clone.sunk | while | flops 3102769152 | bytes 235223312 | solution.py:287
  954.3 6.5 copy-done
  965.0 13.6 fusion.179
  978.6 13.9 fusion.180
  1003.2 6.5 copy-done
  1013.9 13.6 fusion.179
  1027.5 13.9 fusion.180
  1054.6 97.9 %while.69 = (s32[]{:T(128)}, f32[3072,64]{0,1:T(8,128)S(1)}, f32[3072,64]{0,1:T(8,128)}, f32[2,512,3,64]{1,3,2,0:T(8,128)S(1)}, s32[3072]{0:T(1024)S(1)}, /*inde...) while((s32[]{:T(128)}, f32[3072,64]{0,1:T(8,128)S(1)}, ...), condition=%wide.region_16.16_spmd.clone, body=%wide.region_14.15_spmd.clone.sunk | while | flops 3102769152 | bytes 235223312 | solution.py:287
  1060.4 6.5 copy-done
  1071.1 13.6 fusion.179
  1084.7 13.9 fusion.180
  1109.3 6.5 copy-done
  1120.0 13.6 fusion.179
  1133.7 13.9 fusion.180
  1165.3 16.5 collective-permute-done.9
  1181.8 33.4 %collective-permute-done.10 = bf16[1024,3,64]{0,2,1:T(8,128)(2,1)S(1)} collective-permute-done((bf16[1024,3,64]{0,2,1:T(8,128)(2,1)S(1)}, bf16[1024,3,64]{0,2,1:T(8,128)(2,1)S(1)}, u32[]{:S(2)}, u32[]{:S(2)}) %collective-permute-start.10) | collective-permute-done | bytes 393248 | tf_op jit(solution)/shard_map/ppermute | solution.py:42
  1216.5 5.9 fusion.101
  1223.1 13.2 fusion.93
  1236.9 14.7 fusion.91
  1251.7 7.9 convolution_bitcast_fusion.1
  1259.7 54.9 %reduce-scatter.5.cloned.1.call-done = f32[288,3,320]{2,0,1:T(8,128)} async-done(((f32[1152,3,320]{2,0,1:T(8,128)}), f32[288,3,320]{2,0,1:T(8,128)}) %reduce-scatter.5.cloned.1.call-update) | async-done | bytes 1105936 | tf_op jit(solution)/shard_map/reduce_scatter | solution.py:338
  1314.7 126.2 %reduce-scatter.11.cloned.1.call-done = f32[288,1536]{1,0:T(8,128)} async-done(((f32[1152,1536]{1,0:T(8,128)}), f32[288,1536]{1,0:T(8,128)}) %reduce-scatter.11.cloned.1.call-update) | async-done | bytes 1769488 | tf_op jit(solution)/shard_map/reduce_scatter | solution.py:341
  1440.9 240.2 %reduce-scatter.9.cloned.1.call-done = f32[288,2,1536]{2,0,1:T(8,128)} async-done(((f32[1152,2,1536]{2,0,1:T(8,128)}), f32[288,2,1536]{2,0,1:T(8,128)}) %reduce-scatter.9.cloned.1.call-update) | async-done | bytes 3538960 | tf_op jit(solution)/shard_map/reduce_scatter | solution.py:340
  1681.7 122.5 %all-reduce.20.cloned.1.call-done = f32[1024,1152]{1,0:T(8,128)} async-done(((f32[1024,1152]{1,0:T(8,128)}), f32[1024,1152]{1,0:T(8,128)}) %all-reduce.20.cloned.1.call-update) | async-done | bytes 4718608 | tf_op jit(solution)/shard_map/psum | solution.py:329
  1807.8 18.7 all-reduce.4
  1826.7 7.2 all-reduce.5
  1833.9 5.8 fusion.87
  1839.7 107.1 %all-reduce.22.cloned.1.call-done = (f32[288,3,320]{2,0,1:T(8,128)}, f32[288,3,192]{2,0,1:T(8,128)}, f32[288,2,1536]{2,0,1:T(8,128)}, f32[288,1536]{1,0:T(8,128)}) async-done(((f32[288,3,320]{2,0,1:T(8,128)}, f32[288,3,192]{2,0,1:T(8,128)}, f32[288,2,1536]{2,0,1:T(8,128)}, f32[288,1536]{1,0:T(8,128)}), (f32[288,3,320]{2,0,1:T(8,128)}, f32[288,3,192]{2,0,1:T(8,128)}, f32[288,2,1536]{2,0,1:T(8,128)}, ...) | async-done | bytes 7077904 | tf_op jit(solution)/shard_map/psum | solution.py:343
  1946.8 6.7 copy.57
  (389 shorter events, 321.9 us)
Async XLA Ops:
  7.2 14.3 copy-start.45
  7.2 13.7 copy-start.1
  7.2 15.5 copy-start.46
  7.2 15.8 copy-start.47
  7.2 60.9 %all-gather.5.cloned.1.call-start = ((), (), s32[]{:S(2)}) async-start(), calls=%async_computation.4 | async-start | bytes 3317760 | tf_op jit(solution)/shard_map/all_gather | solution.py:100
  7.9 252.2 %all-gather.7.cloned.1.call-start = ((), (), s32[]{:S(2)}) async-start(), calls=%async_computation.5 | async-start | bytes 2211840 | tf_op jit(solution)/shard_map/all_gather | solution.py:101
  8.7 25.7 %collective-permute-start.5 = (bf16[1024]{0:T(1024)(128)(2,1)S(1)}, bf16[1024]{0:T(1024)(128)(2,1)S(1)}, u32[]{:S(2)}, u32[]{:S(2)}) collective-permute-start(bf16[1024]{0:T(1024)(128)(2,1)S(1)} %convert_element_type.101), channel_id=1, source_target_pairs={{0,1},{1,2},{2,3},{4,5},{5,6},{6,7},{8,9},{9,10},{10,11},{12,13},{... | collective-permute-start | bytes 6152 | tf_op jit(solution)/shard_map/ppermute | solution.py:42
  13.6 20.8 %collective-permute-start.4 = (bf16[1024]{0:T(1024)(128)(2,1)S(1)}, bf16[1024]{0:T(1024)(128)(2,1)S(1)}, u32[]{:S(2)}, u32[]{:S(2)}) collective-permute-start(bf16[1024]{0:T(1024)(128)(2,1)S(1)} %convert_element_type.101), channel_id=1, source_target_pairs={{0,2},{1,3},{4,6},{5,7},{8,10},{9,11},{12,14},{13,15},{16,18},{17,... | collective-permute-start | bytes 6152 | tf_op jit(solution)/shard_map/ppermute | solution.py:42
  18.2 387.3 %all-reduce.14.cloned.1.call-start = ((), (), s32[]{:S(2)}) async-start(), calls=%async_computation.6 | async-start | bytes 9437184 | tf_op jit(solution)/shard_map/psum | solution.py:197
  21.4 51.5 %copy-start.38 = (f32[1024]{0:T(1024)}, f32[1024]{0:T(1024)S(1)}, u32[]{:S(2)}) copy-start(f32[1024]{0:T(1024)S(1)} %add_rsqrt_fusion.1) | copy-start | bytes 12292
  24.4 48.8 %copy-start.24 = (f32[1024,32]{0,1:T(8,128)}, f32[1024,32]{0,1:T(8,128)S(1)}, u32[]{:S(2)}) copy-start(f32[1024,32]{0,1:T(8,128)S(1)} %get-tuple-element.776) | copy-start | bytes 393220
  24.4 59.5 %copy-start.10 = (f32[1024,32]{0,1:T(8,128)}, f32[1024,32]{0,1:T(8,128)S(1)}, u32[]{:S(2)}) copy-start(f32[1024,32]{0,1:T(8,128)S(1)} %get-tuple-element.777) | copy-start | bytes 393220
  34.4 38.5 %copy-start.35 = (f32[1152]{0:T(1024)}, f32[1152]{0:T(1024)S(1)}, u32[]{:S(2)}) copy-start(f32[1152]{0:T(1024)S(1)} %convert_element_type.98) | copy-start | bytes 13828
  74.1 19.6 collective-permute-start.1
  75.9 34.7 %collective-permute-start = (bf16[1024,3,64]{0,2,1:T(8,128)(2,1)}, bf16[1024,3,64]{0,2,1:T(8,128)(2,1)}, u32[]{:S(2)}, u32[]{:S(2)}) collective-permute-start(bf16[1024,3,64]{0,2,1:T(8,128)(2,1)} %pad_maximum_fusion.6), channel_id=1, source_target_pairs={{0,2},{1,3},{4,6},{5,7},{8,10},{9,11},{12,14},{13,15},{16,18},{17,... | collective-permute-start | bytes 1179656 | tf_op jit(solution)/shard_map/ppermute | solution.py:42
  80.1 47.3 %collective-permute-start.3 = (bf16[1024,3,64]{0,2,1:T(8,128)(2,1)S(1)}, bf16[1024,3,64]{0,2,1:T(8,128)(2,1)S(1)}, u32[]{:S(2)}, u32[]{:S(2)}) collective-permute-start(bf16[1024,3,64]{0,2,1:T(8,128)(2,1)S(1)} %slice.147), channel_id=1, source_target_pairs={{0,1},{1,2},{2,3},{4,5},{5,6},{6,7},{8,9},{9,10},{10,11},{12,13},{... | collective-permute-start | bytes 1179656 | tf_op jit(solution)/shard_map/ppermute | solution.py:42
  81.8 56.0 %collective-permute-start.2 = (bf16[1024,3,64]{0,2,1:T(8,128)(2,1)S(1)}, bf16[1024,3,64]{0,2,1:T(8,128)(2,1)}, u32[]{:S(2)}, u32[]{:S(2)}) collective-permute-start(bf16[1024,3,64]{0,2,1:T(8,128)(2,1)S(1)} %slice.147), channel_id=1, source_target_pairs={{0,2},{1,3},{4,6},{5,7},{8,10},{9,11},{12,14},{13,15},{16,18},{17,... | collective-permute-start | bytes 1179656 | tf_op jit(solution)/shard_map/ppermute | solution.py:42
  266.6 138.9 %copy-start.2 = (bf16[1024,1152]{1,0:T(8,128)(2,1)S(1)}, bf16[1024,1152]{1,0:T(8,128)(2,1)}, u32[]{:S(2)}) copy-start(bf16[1024,1152]{1,0:T(8,128)(2,1)} %param.18) | copy-start | bytes 7077892
  266.6 269.1 %all-gather.9.cloned.1.call-start = ((), (), s32[]{:S(2)}) async-start(), calls=%async_computation.7 | async-start | bytes 8847360 | tf_op jit(solution)/shard_map/all_gather | solution.py:102
  269.7 335.6 %all-gather.11.cloned.1.call-start = ((), (), s32[]{:S(2)}) async-start(), calls=%async_computation.9 | async-start | bytes 4423680 | tf_op jit(solution)/shard_map/all_gather | solution.py:219
  270.3 475.8 %all-reduce.18.cloned.1.call-start = ((), (), s32[]{:S(2)}) async-start(), calls=%async_computation.10 | async-start | bytes 9437184 | tf_op jit(solution)/shard_map/psum | solution.py:233
  270.4 265.3 %copy-start.25 = (f32[1152]{0:T(1024)}, f32[1152]{0:T(1024)S(1)}, u32[]{:S(2)}) copy-start(f32[1152]{0:T(1024)S(1)} %convert_element_type.105) | copy-start | bytes 13828
  270.4 334.9 %copy-start.42 = (f32[1024]{0:T(1024)}, f32[1024]{0:T(1024)S(1)}, u32[]{:S(2)}) copy-start(f32[1024]{0:T(1024)S(1)} %compare_convert_fusion) | copy-start | bytes 12292
  410.6 407.1 %copy-start.18 = (f32[1024]{0:T(1024)}, f32[1024]{0:T(1024)S(1)}, u32[]{:S(2)}) copy-start(f32[1024]{0:T(1024)S(1)} %add_rsqrt_fusion) | copy-start | bytes 12292
  535.7 69.6 %copy-start.14 = (bf16[1024,1152]{1,0:T(8,128)(2,1)S(1)}, bf16[1024,1152]{1,0:T(8,128)(2,1)}, u32[]{:S(2)}) copy-start(bf16[1024,1152]{1,0:T(8,128)(2,1)} %param.27) | copy-start | bytes 7077892
  605.3 12.8 copy-start.48
  628.1 189.6 %all-reduce.16.cloned.1.call-start = ((), (), s32[]{:S(2)}) async-start(), calls=%async_computation.8 | async-start | bytes 4718592 | tf_op jit(solution)/shard_map/psum | solution.py:208
  629.2 24.3 %collective-permute-start.6 = (bf16[288,1536]{1,0:T(8,128)(2,1)S(1)}, bf16[288,1536]{1,0:T(8,128)(2,1)S(1)}, u32[]{:S(2)}, u32[]{:S(2)}) collective-permute-start(bf16[288,1536]{1,0:T(8,128)(2,1)S(1)} %copy-done.9), channel_id=1, source_target_pairs={{0,1},{1,2},{2,3},{3,0},{4,5},{5,6},{6,7},{7,4},{8,9},{9,10},{10,1... | collective-permute-start | bytes 2654216 | tf_op jit(solution)/shard_map/ppermute | solution.py:30
  629.2 40.2 %collective-permute-start.8 = (bf16[288,1536]{1,0:T(8,128)(2,1)S(1)}, bf16[288,1536]{1,0:T(8,128)(2,1)S(1)}, u32[]{:S(2)}, u32[]{:S(2)}) collective-permute-start(bf16[288,1536]{1,0:T(8,128)(2,1)S(1)} %copy-done.9), channel_id=1, source_target_pairs={{1,0},{2,1},{3,2},{0,3},{5,4},{6,5},{7,6},{4,7},{9,8},{10,9},{11,1... | collective-permute-start | bytes 2654216 | tf_op jit(solution)/shard_map/ppermute | solution.py:32
  653.6 36.7 %copy-start.29 = (bf16[288,1536]{1,0:T(8,128)(2,1)}, bf16[288,1536]{1,0:T(8,128)(2,1)S(1)}, u32[]{:S(2)}) copy-start(bf16[288,1536]{1,0:T(8,128)(2,1)S(1)} %collective-permute-done.6) | copy-start | bytes 2654212
  653.6 36.7 %collective-permute-start.7 = (bf16[288,1536]{1,0:T(8,128)(2,1)S(1)}, bf16[288,1536]{1,0:T(8,128)(2,1)S(1)}, u32[]{:S(2)}, u32[]{:S(2)}) collective-permute-start(bf16[288,1536]{1,0:T(8,128)(2,1)S(1)} %collective-permute-done.6), channel_id=1, source_target_pairs={{0,1},{1,2},{2,3},{3,0},{4,5},{5,6},{6,7},{7,4},{8,9},{9,10},{10,1... | collective-permute-start | bytes 2654216 | tf_op jit(solution)/shard_map/ppermute | solution.py:30
  669.4 20.8 %copy-start.30 = (bf16[288,1536]{1,0:T(8,128)(2,1)}, bf16[288,1536]{1,0:T(8,128)(2,1)S(1)}, u32[]{:S(2)}) copy-start(bf16[288,1536]{1,0:T(8,128)(2,1)S(1)} %collective-permute-done.8) | copy-start | bytes 2654212
  708.9 37.2 %copy-start.26 = (f32[1152]{0:T(1024)S(1)}, f32[1152]{0:T(1024)}, u32[]{:S(2)}) copy-start(f32[1152]{0:T(1024)} %copy-done.25) | copy-start | bytes 13828
  708.9 550.8 %reduce-scatter.7.cloned.1.call-start = ((), (), s32[]{:S(2)}) async-start(), calls=%async_computation.13 | async-start | bytes 4423680 | tf_op jit(solution)/shard_map/reduce_scatter | solution.py:339
  712.5 105.1 %copy-start.15 = (bf16[1024,1152]{1,0:T(8,128)(2,1)S(1)}, bf16[1024,1152]{1,0:T(8,128)(2,1)}, u32[]{:S(2)}) copy-start(bf16[1024,1152]{1,0:T(8,128)(2,1)} %param.27) | copy-start | bytes 7077892
  752.2 74.1 %copy-start.22 = (bf16[1024,3,192]{0,2,1:T(8,128)(2,1)S(1)}, bf16[1024,3,192]{0,2,1:T(8,128)(2,1)}, u32[]{:S(2)}) copy-start(bf16[1024,3,192]{0,2,1:T(8,128)(2,1)} %copy-done.21) | copy-start | bytes 3538948
  836.9 477.7 %reduce-scatter.5.cloned.1.call-start = ((), (), s32[]{:S(2)}) async-start(), calls=%async_computation.12 | async-start | bytes 6635520 | tf_op jit(solution)/shard_map/reduce_scatter | solution.py:338
  845.2 9.1 copy-start.4
  858.6 13.7 copy-start.5
  894.4 9.1 copy-start.4
  907.8 13.6 copy-start.5
  951.6 9.1 copy-start.4
  965.0 13.6 copy-start.5
  1000.5 9.1 copy-start.4
  1013.9 13.6 copy-start.5
  1057.7 9.1 copy-start.4
  1071.1 13.6 copy-start.5
  1106.6 9.1 copy-start.4
  1120.0 13.6 copy-start.5
  1159.5 56.0 %collective-permute-start.11 = (bf16[1024,3,64]{0,2,1:T(8,128)(2,1)S(1)}, bf16[1024,3,64]{0,2,1:T(8,128)(2,1)S(1)}, u32[]{:S(2)}, u32[]{:S(2)}) collective-permute-start(bf16[1024,3,64]{0,2,1:T(8,128)(2,1)S(1)} %get-tuple-element.771), channel_id=1, source_target_pairs={{1,0},{2,1},{3,2},{5,4},{6,5},{7,6},{9,8},{10,9},{11,10},{13,12},{... | collective-permute-start | bytes 1179656 | tf_op jit(solution)/shard_map/ppermute | solution.py:42
  1160.8 54.7 %collective-permute-start.12 = (bf16[1024,3,64]{0,2,1:T(8,128)(2,1)S(1)}, bf16[1024,3,64]{0,2,1:T(8,128)(2,1)S(1)}, u32[]{:S(2)}, u32[]{:S(2)}) collective-permute-start(bf16[1024,3,64]{0,2,1:T(8,128)(2,1)S(1)} %get-tuple-element.772), channel_id=1, source_target_pairs={{2,0},{3,1},{6,4},{7,5},{10,8},{11,9},{14,12},{15,13},{18,16},{19,... | collective-permute-start | bytes 1179656 | tf_op jit(solution)/shard_map/ppermute | solution.py:42
  1162.2 19.6 collective-permute-start.9
  1163.5 51.7 %collective-permute-start.10 = (bf16[1024,3,64]{0,2,1:T(8,128)(2,1)S(1)}, bf16[1024,3,64]{0,2,1:T(8,128)(2,1)S(1)}, u32[]{:S(2)}, u32[]{:S(2)}) collective-permute-start(bf16[1024,3,64]{0,2,1:T(8,128)(2,1)S(1)} %get-tuple-element.770), channel_id=1, source_target_pairs={{2,0},{3,1},{6,4},{7,5},{10,8},{11,9},{14,12},{15,13},{18,16},{19,... | collective-permute-start | bytes 1179656 | tf_op jit(solution)/shard_map/ppermute | solution.py:42
  1165.2 51.3 %copy-start.3 = (bf16[1024,1152]{1,0:T(8,128)(2,1)S(1)}, bf16[1024,1152]{1,0:T(8,128)(2,1)}, u32[]{:S(2)}) copy-start(bf16[1024,1152]{1,0:T(8,128)(2,1)} %param.18) | copy-start | bytes 7077892
  1165.2 51.3 %copy-start.36 = (f32[1152]{0:T(1024)S(1)}, f32[1152]{0:T(1024)}, u32[]{:S(2)}) copy-start(f32[1152]{0:T(1024)} %copy-done.35) | copy-start | bytes 13828
  1165.2 51.3 %copy-start.39 = (f32[1024]{0:T(1024)S(1)}, f32[1024]{0:T(1024)}, u32[]{:S(2)}) copy-start(f32[1024]{0:T(1024)} %copy-done.38) | copy-start | bytes 12292
  1222.4 218.5 %reduce-scatter.11.cloned.1.call-start = ((), (), s32[]{:S(2)}) async-start(), calls=%async_computation.15 | async-start | bytes 8847360 | tf_op jit(solution)/shard_map/reduce_scatter | solution.py:341
  1236.3 444.8 %reduce-scatter.9.cloned.1.call-start = ((), (), s32[]{:S(2)}) async-start(), calls=%async_computation.14 | async-start | bytes 17694720 | tf_op jit(solution)/shard_map/reduce_scatter | solution.py:340
  1251.7 552.5 %all-reduce.20.cloned.1.call-start = ((), (), s32[]{:S(2)}) async-start(), calls=%async_computation.11 | async-start | bytes 9437184 | tf_op jit(solution)/shard_map/psum | solution.py:329
  1259.7 687.1 %all-reduce.22.cloned.1.call-start = ((), (), s32[]{:S(2)}) async-start(), calls=%async_computation.16 | async-start | bytes 15040512 | tf_op jit(solution)/shard_map/psum | solution.py:343
  1681.0 123.2 %copy-start.37 = (f32[1152]{0:T(1024)S(1)}, f32[1152]{0:T(1024)}, u32[]{:S(2)}) copy-start(f32[1152]{0:T(1024)} %copy-done.35) | copy-start | bytes 13828
  1681.7 126.1 %copy-start.41 = (f32[1152]{0:T(1024)S(1)}, f32[1152]{0:T(1024)}, u32[]{:S(2)}) copy-start(f32[1152]{0:T(1024)} %get-tuple-element.623) | copy-start | bytes 13828
  1946.8 6.7 copy-start.20
  1946.8 7.7 copy-start.28
  (26 other events, 85.9 us)
Sparse Core Ops, SparseCore 0:
  9.6 58.4 all-gather.4
  69.7 63.9 all-gather.6
  266.7 138.7 all-reduce.13
  407.5 128.1 all-gather.8
  537.1 68.1 all-gather.10
  628.2 117.8 all-reduce.17
  749.0 68.6 all-reduce.15
  837.1 66.4 reduce-scatter.6
  1222.5 92.0 reduce-scatter.4
  1316.8 124.0 reduce-scatter.10
  1443.2 237.7 reduce-scatter.8
  1683.9 120.2 all-reduce.19
  1806.9 139.9 all-reduce.21
